TPU v7x, 32 devices: a whole 2x2x4 slice. The times are simulated.
32 devices in a mesh: run: 8 (over z, core), mz: 4 (over y, x).
Axes of the slice: x: 2, y: 2, z: 4, core: 2. Of those that a mesh axis runs over, the one named last changes fastest.
Arguments:
- lcms: bfloat16 [512, 256, 4096], P('run', None, 'mz'), may hold values from -600 to 600
- spectra: float32 [512, 65536], P('run', 'mz'), may hold values from -200 to 200
- scan_factor: float32 [64, 256], replicated, may hold values from 0.05 to 0.9
- mz_factor: float32 [64, 4096], P(None, 'mz'), may hold values from 0 to 1.7
- ppm_factor: float32 [64, 65536], P(None, 'mz'), may hold values from 0 to 1.7
Outputs:
- sample_factor: float32 [512, 64], P('run')
- ppm_new: float32 [64, 65536], P(None, ('mz', 'run'))
All inputs are finite; a program needn't handle non-finite values.
Results may differ from a plain program's by a relative error of at most 0.0048.
Values sent between devices are 32-bit elements; how exact they have to be, the bound alone decides.
No kernel may reach another device: no remote copies, remote signals or barrier semaphores. Data moves between devices by JAX's collectives and lax.ppermute only.
A program may use at most 128 MiB of HBM per device.

v0:
```python
import jax
import jax.numpy as jnp
from jax import lax
from jax.sharding import PartitionSpec as P


def solve_rows(gram_matrix, right_rows):
    lower_factor = jnp.linalg.cholesky(gram_matrix)
    return jax.scipy.linalg.cho_solve((lower_factor, True), right_rows.T).T


def per_device(lcms, spectra, scan_factor, mz_factor, ppm_factor):
    highest = lax.Precision.HIGHEST
    shared_spectra = lax.all_to_all(spectra, "run", split_axis=1, concat_axis=0, tiled=True)
    scan_bf = scan_factor.astype(jnp.bfloat16)
    tensor = jnp.einsum("ijk,rj->irk", lcms, scan_bf, preferred_element_type=jnp.float32)
    lcms_local = jnp.sum(tensor * mz_factor[None], axis=2)
    nmr_local = lax.dot_general(spectra, ppm_factor, (((1,), (1,)), ((), ())), precision=highest)
    mz_local = jnp.dot(mz_factor, mz_factor.T, precision=highest)
    ppm_local = jnp.dot(ppm_factor, ppm_factor.T, precision=highest)
    mz_gram, ppm_gram = lax.psum((mz_local, ppm_local), "mz")
    lcms_part, nmr_part = lax.psum((lcms_local, nmr_local), "mz")
    lcms_gram = jnp.dot(scan_factor, scan_factor.T, precision=highest) * mz_gram
    sample_first = solve_rows(lcms_gram + ppm_gram, lcms_part + nmr_part)
    whole_rows = lax.all_gather(sample_first, "run", axis=0, tiled=True)
    sample_gram = lax.psum(jnp.dot(sample_first.T, sample_first, precision=highest), "run")
    projected = jnp.dot(whole_rows.T, shared_spectra, precision=highest)
    ppm_new = jax.scipy.linalg.cho_solve((jnp.linalg.cholesky(sample_gram), True), projected)
    gram_local = jnp.dot(ppm_new, ppm_new.T, precision=highest)
    new_gram = lax.psum(gram_local, ("run", "mz"))
    fit_local = lax.dot_general(
        shared_spectra, ppm_new, (((1,), (1,)), ((), ())), precision=highest
    )
    fit_owned = lax.psum_scatter(fit_local, "run", scatter_dimension=0, tiled=True)
    nmr_fit = lax.psum(fit_owned, "mz")
    sample_factor = solve_rows(lcms_gram + new_gram, lcms_part + nmr_fit)
    return (sample_factor, ppm_new)


def solution(mesh):
    return jax.shard_map(
        per_device,
        mesh=mesh,
        in_specs=(P("run", None, "mz"), P("run", "mz"), P(), P(None, "mz"), P(None, "mz")),
        out_specs=(P("run", None), P(None, ("mz", "run"))),
        check_vma=False,
    )
```

profile of v0, /device:TPU:0, one launch (start us, length us, event | category | flops | bytes accessed | tf_op | source)
XLA Modules:
  0.0 250.2 jit_solution(10968291417373203832)
XLA Ops:
  7.2 4.7 %copy.56 = f32[8,8,8,2048]{3,2,0,1:T(8,128)} copy(f32[8,8,8,2048]{3,2,1,0:T(8,128)} %bitcast.76) | data formatting | bytes 8388608 | tf_op jit(solution)/shard_map/all_to_all | solution.py:14
  11.8 6.5 %all-to-all-start = ((f32[64,8,2048]{2,0,1:T(8,128)}), f32[64,8,2048]{2,0,1:T(8,128)}, u32[]{:S(2)}, u32[]{:S(2)}) async-start(f32[64,8,2048]{2,0,1:T(8,128)} %bitcast.77), calls=%async_computation | async-start | bytes 8388608 | tf_op jit(solution)/shard_map/all_to_all | solution.py:14
  18.4 1.0 fusion.28
  19.3 7.7 %fusion.30 = f32[64,64]{1,0:T(8,128)} fusion(f32[64,16384]{1,0:T(8,128)} %param.9, f32[64,16384]{1,0:T(8,128)} %param.12), kind=kOutput, calls=%fused_computation.47 | convolution fusion | flops 805306368 | bytes 8404992 | tf_op jit(solution)/shard_map/dot_general | solution.py:18
  27.0 4.0 %fusion.29 = f32[64,64]{0,1:T(8,128)} fusion(f32[64,16384]{1,0:T(8,128)S(1)} %copy-done), kind=kOutput, calls=%fused_computation.46 | convolution fusion | flops 805306368 | bytes 4210688 | tf_op jit(solution)/shard_map/dot_general | solution.py:20
  31.0 17.2 %multiply_reduce_fusion = f32[64,64]{0,1:T(8,128)} fusion(bf16[64,256,1024]{2,1,0:T(8,128)(2,1)} %param.8, f32[64,1024]{1,0:T(8,128)S(1)} %copy-done.2, f32[64,256]{1,0:T(8,128)S(1)} %copy-done.3), kind=kOutput, calls=%fused_computation | convolution fusion | flops 2155884544 | bytes 33898496 | tf_op jit(solution)/shard_map/ijk,rj->irk/dot_general | solution.py:16
  48.4 44.0 %all-reduce.3.cloned.1.call-done = (f32[64,64]{0,1:T(8,128)}, f32[64,64]{0,1:T(8,128)}, f32[64,64]{1,0:T(8,128)}, f32[64,64]{1,0:T(8,128)}) async-done(((f32[64,64]{0,1:T(8,128)}, f32[64,64]{0,1:T(8,128)}, f32[64,64]{1,0:T(8,128)}, f32[64,64]{1,0:T(8,128)}), (f32[64,64]{0,1:T(8,128)}, f32[64,64]{0,1:T(8,128)}, f32[64,64]{1,0:T(8,128)}, f32[64,64]{1,0:T(8,128)})) %all-reduce.3.cloned.1.call-update) | async-done | bytes 65552 | tf_op jit(solution)/shard_map/psum | solution.py:21
  92.4 1.0 fusion.27
  93.5 5.8 %cholesky.59 = f32[64,64]{1,0:T(8,128)S(1)} custom-call(f32[64,64]{1,0:T(8,128)S(1)} %fusion.19), custom_call_target="Cholesky" | custom-call | tf_op jit(solution)/shard_map/jit(cholesky)/cholesky | solution.py:8
  100.0 0.7 fusion
  100.7 4.9 %custom-call.16 = f32[1,64,64]{1,2,0:T(8,128)S(1)} custom-call(f32[1,64,64]{2,1,0:T(8,128)S(1)} %fusion), custom_call_target="InvertDiagBlocksLowerTriangular" | custom-call | tf_op jit(solution)/shard_map/jit(_cho_solve)/triangular_solve | solution.py:9
  105.6 1.0 fusion.13
  107.1 28.0 %psum.53 = f32[64,64]{0,1:T(8,128)S(1)} all-reduce(f32[64,64]{0,1:T(8,128)S(1)} %fusion.31), channel_id=1, replica_groups=mesh['run'=8,'mz'=4] {'run'}, use_global_device_ids=true, to_apply=%region_7.10 | all-reduce | flops 4096 | bytes 32768 | tf_op jit(solution)/shard_map/psum | solution.py:26
  135.2 5.8 %cholesky.70 = f32[64,64]{1,0:T(8,128)S(1)} custom-call(f32[64,64]{1,0:T(8,128)S(1)} %fusion.12), custom_call_target="Cholesky" | custom-call | tf_op jit(solution)/shard_map/jit(cholesky)/cholesky | solution.py:28
  142.4 4.9 %custom-call.14 = f32[1,64,64]{1,2,0:T(8,128)S(1)} custom-call(f32[1,64,64]{2,1,0:T(8,128)S(1)} %fusion.1), custom_call_target="InvertDiagBlocksLowerTriangular" | custom-call | tf_op jit(solution)/shard_map/jit(_cho_solve)/triangular_solve | solution.py:28
  147.3 14.2 %all_gather.3 = f32[512,64]{1,0:T(8,128)S(1)} all-gather(f32[64,64]{1,0:T(8,128)S(1)} %copy.42), channel_id=1, replica_groups=mesh['run'=8,'mz'=4] {'run'}, dimensions={0}, use_global_device_ids=true | all-gather | bytes 147456 | tf_op jit(solution)/shard_map/all_gather | solution.py:25
  161.5 4.8 %fusion.32 = f32[64,2048]{1,0:T(8,128)S(1)} fusion(f32[512,64]{1,0:T(8,128)S(1)} %all_gather.3, f32[512,2048]{1,0:T(8,128)} %bitcast.11), kind=kOutput, calls=%fused_computation.49 | convolution fusion | flops 805306368 | bytes 4849664 | tf_op jit(solution)/shard_map/dot_general | solution.py:27
  167.5 6.5 %convolution_bitcast_fusion = f32[512,64]{1,0:T(8,128)} fusion(f32[64,2048]{1,0:T(8,128)S(1)} %fusion.8, f32[512,2048]{1,0:T(8,128)} %bitcast.11), kind=kOutput, calls=%fused_computation.2 | convolution fusion | flops 805306368 | bytes 4849664 | tf_op jit(solution)/shard_map/dot_general | solution.py:31
  174.6 37.8 %psum.54 = f32[64,64]{0,1:T(8,128)S(1)} all-reduce(f32[64,64]{0,1:T(8,128)S(1)} %fusion.33), channel_id=1, replica_groups=mesh['run'=8,'mz'=4] {'run','mz'}, use_global_device_ids=true, to_apply=%region_8.11 | all-reduce | flops 4096 | bytes 32768 | tf_op jit(solution)/shard_map/psum | solution.py:30
  212.5 5.8 %cholesky.81 = f32[64,64]{1,0:T(8,128)S(1)} custom-call(f32[64,64]{1,0:T(8,128)S(1)} %fusion.7), custom_call_target="Cholesky" | custom-call | tf_op jit(solution)/shard_map/jit(cholesky)/cholesky | solution.py:8
  219.0 0.7 fusion.2
  219.7 4.9 %custom-call.17 = f32[1,64,64]{1,2,0:T(8,128)S(1)} custom-call(f32[1,64,64]{2,1,0:T(8,128)S(1)} %fusion.2), custom_call_target="InvertDiagBlocksLowerTriangular" | custom-call | tf_op jit(solution)/shard_map/jit(_cho_solve)/triangular_solve | solution.py:9
  224.6 17.7 %psum.55 = f32[64,64]{1,0:T(8,128)S(1)} all-reduce(f32[64,64]{1,0:T(8,128)} %reduce-scatter.2.cloned.1.call-done), channel_id=1, replica_groups=mesh['run'=8,'mz'=4] {'mz'}, use_global_device_ids=true, to_apply=%region_10.13 | all-reduce | flops 4096 | bytes 32768 | tf_op jit(solution)/shard_map/psum | solution.py:35
  242.7 0.7 copy.47
  (38 shorter events, 5.9 us)
Async XLA Ops:
  11.8 6.5 %copy-start.2 = (f32[64,1024]{1,0:T(8,128)S(1)}, f32[64,1024]{1,0:T(8,128)}, u32[]{:S(2)}) copy-start(f32[64,1024]{1,0:T(8,128)} %param.11) | copy-start | bytes 786436
  11.8 149.6 %all-to-all-start = ((f32[64,8,2048]{2,0,1:T(8,128)}), f32[64,8,2048]{2,0,1:T(8,128)}, u32[]{:S(2)}, u32[]{:S(2)}) async-start(f32[64,8,2048]{2,0,1:T(8,128)} %bitcast.77), calls=%async_computation | async-start | bytes 8388608 | tf_op jit(solution)/shard_map/all_to_all | solution.py:14
  18.3 74.1 %all-reduce.3.cloned.1.call-start = ((), (), s32[]{:S(2)}) async-start(), calls=%async_computation.3 | async-start | bytes 262144 | tf_op jit(solution)/shard_map/psum | solution.py:21
  19.3 7.7 %copy-start = (f32[64,16384]{1,0:T(8,128)S(1)}, f32[64,16384]{1,0:T(8,128)}, u32[]{:S(2)}) copy-start(f32[64,16384]{1,0:T(8,128)} %param.12) | copy-start | bytes 12582916
  27.0 4.0 %copy-start.3 = (f32[64,256]{1,0:T(8,128)S(1)}, f32[64,256]{1,0:T(8,128)}, u32[]{:S(2)}) copy-start(f32[64,256]{1,0:T(8,128)} %param.10) | copy-start | bytes 196612
  48.2 176.4 %reduce-scatter.2.cloned.1.call-start = ((), (), s32[]{:S(2)}) async-start(), calls=%async_computation.2 | async-start | bytes 294912 | tf_op jit(solution)/shard_map/reduce_scatter | solution.py:34
  166.9 75.4 %copy-start.4 = (f32[64,64]{1,0:T(8,128)S(1)}, f32[64,64]{1,0:T(8,128)}, u32[]{:S(2)}) copy-start(f32[64,64]{1,0:T(8,128)} %get-tuple-element.14) | copy-start | bytes 49156
  167.5 75.9 %copy-start.1 = (f32[64,2048]{1,0:T(8,128)}, f32[64,2048]{1,0:T(8,128)S(1)}, u32[]{:S(2)}) copy-start(f32[64,2048]{1,0:T(8,128)S(1)} %fusion.8) | copy-start | bytes 1572868
Sparse Core Ops, SparseCore 0:
  48.3 44.0 all-reduce.2
  174.7 28.0 reduce-scatter.1
where the time goes:
time: 251 us; the launch traced here: 250 us
  blocking collectives  97.7 us (39%)
  matrix products  45.6 us (18%)
  waiting for transfers between devices  44.1 us (18%)
  other arithmetic  36.2 us (14%)
  between operations  14.2 us (6%)
  starting transfers between devices  6.74 us (3%)
  local copies, waits for them, and re-layouts  5.68 us (2%)
    psum x1, waiting for transfers between devices, per_device(): mz_gram, ppm_gram = lax.psum((mz_local, ppm_local), 'mz')  44 us
    psum x1, blocking collectives, per_device(): new_gram = lax.psum(gram_local, ('run', 'mz'))  37.8 us
    psum x1, blocking collectives, per_device(): lax.psum(jnp.dot(sample_first.T, sample_first, precision=highest), 'run')  28 us
    psum x1, blocking collectives, per_device(): nmr_fit = lax.psum(fit_owned, 'mz')  17.7 us
    dot_general x1, matrix products, per_device(): jnp.einsum('ijk,rj->irk', lcms, scan_bf, preferred_element_type=jnp.float32)  17.2 us
    all_gather x1, blocking collectives, per_device(): whole_rows = lax.all_gather(sample_first, 'run', axis=0, tiled=True)  14.2 us
    another operation x6, other arithmetic, solve_rows(): lower_factor = jnp.linalg.cholesky(gram_matrix)  13 us
    another operation x4, other arithmetic, solve_rows(): return jax.scipy.linalg.cho_solve((lower_factor, True), right_rows.T).T  11.1 us
  transfers between devices with their start and end apart: 3, of which 1 were waited for; matrix products, arithmetic and copies ran while one was open for 27% of the time, Pallas kernels for 0%

commit v1 on v0

--- a/solution.py
+++ b/solution.py
@@ -27,7 +27,8 @@
     projected = jnp.dot(whole_rows.T, shared_spectra, precision=highest)
     ppm_new = jax.scipy.linalg.cho_solve((jnp.linalg.cholesky(sample_gram), True), projected)
     gram_local = jnp.dot(ppm_new, ppm_new.T, precision=highest)
-    new_gram = lax.psum(gram_local, ("run", "mz"))
+    one_axis = lax.psum(gram_local, "mz")
+    new_gram = lax.psum(one_axis, "run")
     fit_local = lax.dot_general(
         shared_spectra, ppm_new, (((1,), (1,)), ((), ())), precision=highest
     )

time: 251 us -> 266 us (1.060)
  waiting for transfers between devices: 44.1 us -> 71.6 us
  blocking collectives: 97.7 us -> 85.6 us
    reduce_scatter x1, waiting for transfers between devices: 0.03 us -> 27.6 us  [per_device(): lax.psum_scatter(fit_local, 'run', scatter_dimension=0, tiled=True)]
    psum x2, blocking collectives: 55.5 us -> 43.4 us  [the longest x1 25.9 us: per_device(): new_gram = lax.psum(one_axis, 'run')]
  transfers between devices with their start and end apart: 3 -> 3, of which waited for: 1 -> 2; matrix products, arithmetic and copies ran while one was open for 27% -> 21% of each run, Pallas kernels for 0% -> 0%
where the time goes in v1:
time: 266 us
  blocking collectives  85.6 us (32%)
  waiting for transfers between devices  71.6 us (27%)
  matrix products  45.6 us (17%)
  other arithmetic  36.2 us (14%)
  between operations  14.2 us (5%)
  starting transfers between devices  6.74 us (3%)
  local copies, waits for them, and re-layouts  5.69 us (2%)
    psum x1, waiting for transfers between devices, per_device(): mz_gram, ppm_gram = lax.psum((mz_local, ppm_local), 'mz')  44 us
    psum x1, blocking collectives, per_device(): lax.psum(jnp.dot(sample_first.T, sample_first, precision=highest), 'run')  28 us
    reduce_scatter x1, waiting for transfers between devices, per_device(): lax.psum_scatter(fit_local, 'run', scatter_dimension=0, tiled=True)  27.6 us
    psum x1, blocking collectives, per_device(): new_gram = lax.psum(one_axis, 'run')  25.9 us
    psum x1, blocking collectives, per_device(): one_axis = lax.psum(gram_local, 'mz')  17.4 us
    dot_general x1, matrix products, per_device(): jnp.einsum('ijk,rj->irk', lcms, scan_bf, preferred_element_type=jnp.float32)  17.2 us
    all_gather x1, blocking collectives, per_device(): whole_rows = lax.all_gather(sample_first, 'run', axis=0, tiled=True)  14.2 us
    another operation x6, other arithmetic, solve_rows(): lower_factor = jnp.linalg.cholesky(gram_matrix)  13 us
  transfers between devices with their start and end apart: 3, of which 2 were waited for; matrix products, arithmetic and copies ran while one was open for 21% of the time, Pallas kernels for 0%

profile of v1, /device:TPU:0, one launch (start us, length us, event | category | flops | bytes accessed | tf_op | source)
XLA Modules:
  0.0 265.7 jit_solution(4890407910668177663)
XLA Ops:
  7.2 4.7 %copy.56 = f32[8,8,8,2048]{3,2,0,1:T(8,128)} copy(f32[8,8,8,2048]{3,2,1,0:T(8,128)} %bitcast.76) | data formatting | bytes 8388608 | tf_op jit(solution)/shard_map/all_to_all | solution.py:14
  11.8 6.5 %all-to-all-start = ((f32[64,8,2048]{2,0,1:T(8,128)}), f32[64,8,2048]{2,0,1:T(8,128)}, u32[]{:S(2)}, u32[]{:S(2)}) async-start(f32[64,8,2048]{2,0,1:T(8,128)} %bitcast.77), calls=%async_computation | async-start | bytes 8388608 | tf_op jit(solution)/shard_map/all_to_all | solution.py:14
  18.4 1.0 fusion.28
  19.3 7.7 %fusion.30 = f32[64,64]{1,0:T(8,128)} fusion(f32[64,16384]{1,0:T(8,128)} %param.9, f32[64,16384]{1,0:T(8,128)} %param.12), kind=kOutput, calls=%fused_computation.47 | convolution fusion | flops 805306368 | bytes 8404992 | tf_op jit(solution)/shard_map/dot_general | solution.py:18
  27.0 4.0 %fusion.29 = f32[64,64]{0,1:T(8,128)} fusion(f32[64,16384]{1,0:T(8,128)S(1)} %copy-done), kind=kOutput, calls=%fused_computation.46 | convolution fusion | flops 805306368 | bytes 4210688 | tf_op jit(solution)/shard_map/dot_general | solution.py:20
  31.0 17.2 %multiply_reduce_fusion = f32[64,64]{0,1:T(8,128)} fusion(bf16[64,256,1024]{2,1,0:T(8,128)(2,1)} %param.8, f32[64,1024]{1,0:T(8,128)S(1)} %copy-done.2, f32[64,256]{1,0:T(8,128)S(1)} %copy-done.3), kind=kOutput, calls=%fused_computation | convolution fusion | flops 2155884544 | bytes 33898496 | tf_op jit(solution)/shard_map/ijk,rj->irk/dot_general | solution.py:16
  48.4 44.0 %all-reduce.4.cloned.1.call-done = (f32[64,64]{0,1:T(8,128)}, f32[64,64]{0,1:T(8,128)}, f32[64,64]{1,0:T(8,128)}, f32[64,64]{1,0:T(8,128)}) async-done(((f32[64,64]{0,1:T(8,128)}, f32[64,64]{0,1:T(8,128)}, f32[64,64]{1,0:T(8,128)}, f32[64,64]{1,0:T(8,128)}), (f32[64,64]{0,1:T(8,128)}, f32[64,64]{0,1:T(8,128)}, f32[64,64]{1,0:T(8,128)}, f32[64,64]{1,0:T(8,128)})) %all-reduce.4.cloned.1.call-update) | async-done | bytes 65552 | tf_op jit(solution)/shard_map/psum | solution.py:21
  92.4 1.0 fusion.27
  93.5 5.8 %cholesky.59 = f32[64,64]{1,0:T(8,128)S(1)} custom-call(f32[64,64]{1,0:T(8,128)S(1)} %fusion.19), custom_call_target="Cholesky" | custom-call | tf_op jit(solution)/shard_map/jit(cholesky)/cholesky | solution.py:8
  100.0 0.7 fusion
  100.7 4.9 %custom-call.16 = f32[1,64,64]{1,2,0:T(8,128)S(1)} custom-call(f32[1,64,64]{2,1,0:T(8,128)S(1)} %fusion), custom_call_target="InvertDiagBlocksLowerTriangular" | custom-call | tf_op jit(solution)/shard_map/jit(_cho_solve)/triangular_solve | solution.py:9
  105.6 1.0 fusion.13
  107.1 28.0 %psum.60 = f32[64,64]{0,1:T(8,128)S(1)} all-reduce(f32[64,64]{0,1:T(8,128)S(1)} %fusion.31), channel_id=1, replica_groups=mesh['run'=8,'mz'=4] {'run'}, use_global_device_ids=true, to_apply=%region_7.10 | all-reduce | flops 4096 | bytes 32768 | tf_op jit(solution)/shard_map/psum | solution.py:26
  135.2 5.8 %cholesky.70 = f32[64,64]{1,0:T(8,128)S(1)} custom-call(f32[64,64]{1,0:T(8,128)S(1)} %fusion.12), custom_call_target="Cholesky" | custom-call | tf_op jit(solution)/shard_map/jit(cholesky)/cholesky | solution.py:28
  142.4 4.9 %custom-call.14 = f32[1,64,64]{1,2,0:T(8,128)S(1)} custom-call(f32[1,64,64]{2,1,0:T(8,128)S(1)} %fusion.1), custom_call_target="InvertDiagBlocksLowerTriangular" | custom-call | tf_op jit(solution)/shard_map/jit(_cho_solve)/triangular_solve | solution.py:28
  147.3 14.2 %all_gather.3 = f32[512,64]{1,0:T(8,128)S(1)} all-gather(f32[64,64]{1,0:T(8,128)S(1)} %copy.42), channel_id=1, replica_groups=mesh['run'=8,'mz'=4] {'run'}, dimensions={0}, use_global_device_ids=true | all-gather | bytes 147456 | tf_op jit(solution)/shard_map/all_gather | solution.py:25
  161.5 4.8 %fusion.32 = f32[64,2048]{1,0:T(8,128)S(1)} fusion(f32[512,64]{1,0:T(8,128)S(1)} %all_gather.3, f32[512,2048]{1,0:T(8,128)} %bitcast.11), kind=kOutput, calls=%fused_computation.49 | convolution fusion | flops 805306368 | bytes 4849664 | tf_op jit(solution)/shard_map/dot_general | solution.py:27
  167.5 6.5 %convolution_bitcast_fusion = f32[512,64]{1,0:T(8,128)} fusion(f32[64,2048]{1,0:T(8,128)S(1)} %fusion.8, f32[512,2048]{1,0:T(8,128)} %bitcast.11), kind=kOutput, calls=%fused_computation.2 | convolution fusion | flops 805306368 | bytes 4849664 | tf_op jit(solution)/shard_map/dot_general | solution.py:32
  174.6 27.6 %reduce-scatter.2.cloned.1.call-done = f32[64,64]{1,0:T(8,128)} async-done(((f32[512,64]{1,0:T(8,128)}), f32[64,64]{1,0:T(8,128)}) %reduce-scatter.2.cloned.1.call-update) | async-done | bytes 16400 | tf_op jit(solution)/shard_map/reduce_scatter | solution.py:35
  202.2 17.4 %all-reduce = (f32[64,64]{0,1:T(8,128)S(1)}, f32[64,64]{1,0:T(8,128)S(1)}) all-reduce(f32[64,64]{0,1:T(8,128)S(1)} %fusion.33, f32[64,64]{1,0:T(8,128)} %reduce-scatter.2.cloned.1.call-done), channel_id=1, replica_groups=mesh['run'=8,'mz'=4] {'mz'}, use_global_device_ids=true, to_apply=%region_8.11 | all-reduce | flops 8192 | bytes 65536 | tf_op jit(solution)/shard_map/psum | solution.py:30
  219.6 25.9 %psum.62 = f32[64,64]{0,1:T(8,128)S(1)} all-reduce(f32[64,64]{0,1:T(8,128)S(1)} %get-tuple-element.12), channel_id=1, replica_groups=mesh['run'=8,'mz'=4] {'run'}, use_global_device_ids=true, to_apply=%region_9.12 | all-reduce | flops 4096 | bytes 32768 | tf_op jit(solution)/shard_map/psum | solution.py:31
  245.7 5.8 %cholesky.81 = f32[64,64]{1,0:T(8,128)S(1)} custom-call(f32[64,64]{1,0:T(8,128)S(1)} %fusion.7), custom_call_target="Cholesky" | custom-call | tf_op jit(solution)/shard_map/jit(cholesky)/cholesky | solution.py:8
  252.9 4.9 %custom-call.17 = f32[1,64,64]{1,2,0:T(8,128)S(1)} custom-call(f32[1,64,64]{2,1,0:T(8,128)S(1)} %fusion.2), custom_call_target="InvertDiagBlocksLowerTriangular" | custom-call | tf_op jit(solution)/shard_map/jit(_cho_solve)/triangular_solve | solution.py:9
  258.2 0.7 copy.47
  (38 shorter events, 6.5 us)
Async XLA Ops:
  11.8 6.5 %copy-start.2 = (f32[64,1024]{1,0:T(8,128)S(1)}, f32[64,1024]{1,0:T(8,128)}, u32[]{:S(2)}) copy-start(f32[64,1024]{1,0:T(8,128)} %param.11) | copy-start | bytes 786436
  11.8 149.6 %all-to-all-start = ((f32[64,8,2048]{2,0,1:T(8,128)}), f32[64,8,2048]{2,0,1:T(8,128)}, u32[]{:S(2)}, u32[]{:S(2)}) async-start(f32[64,8,2048]{2,0,1:T(8,128)} %bitcast.77), calls=%async_computation | async-start | bytes 8388608 | tf_op jit(solution)/shard_map/all_to_all | solution.py:14
  18.3 74.1 %all-reduce.4.cloned.1.call-start = ((), (), s32[]{:S(2)}) async-start(), calls=%async_computation.3 | async-start | bytes 262144 | tf_op jit(solution)/shard_map/psum | solution.py:21
  19.3 7.7 %copy-start = (f32[64,16384]{1,0:T(8,128)S(1)}, f32[64,16384]{1,0:T(8,128)}, u32[]{:S(2)}) copy-start(f32[64,16384]{1,0:T(8,128)} %param.12) | copy-start | bytes 12582916
  27.0 4.0 %copy-start.3 = (f32[64,256]{1,0:T(8,128)S(1)}, f32[64,256]{1,0:T(8,128)}, u32[]{:S(2)}) copy-start(f32[64,256]{1,0:T(8,128)} %param.10) | copy-start | bytes 196612
  48.2 154.0 %reduce-scatter.2.cloned.1.call-start = ((), (), s32[]{:S(2)}) async-start(), calls=%async_computation.2 | async-start | bytes 294912 | tf_op jit(solution)/shard_map/reduce_scatter | solution.py:35
  166.9 90.9 %copy-start.4 = (f32[64,64]{1,0:T(8,128)S(1)}, f32[64,64]{1,0:T(8,128)}, u32[]{:S(2)}) copy-start(f32[64,64]{1,0:T(8,128)} %get-tuple-element.16) | copy-start | bytes 49156
  167.5 91.4 %copy-start.1 = (f32[64,2048]{1,0:T(8,128)}, f32[64,2048]{1,0:T(8,128)S(1)}, u32[]{:S(2)}) copy-start(f32[64,2048]{1,0:T(8,128)S(1)} %fusion.8) | copy-start | bytes 1572868
Sparse Core Ops, SparseCore 0:
  48.3 44.0 all-reduce.3
  174.1 28.0 reduce-scatter.1
